TPU v7x, 512 devices: a whole 4x4x16 slice. The times are simulated.
512 devices in a mesh: slab: 128 (over y, z, core), tile: 4 (over x).
Axes of the slice: x: 4, y: 4, z: 16, core: 2. Of those that a mesh axis runs over, the one named last changes fastest.
Arguments:
- tokens: bfloat16 [1024, 1024, 128], P('slab', 'tile'), may hold values from -6 to 6
- conv_weight: float32 [3, 3, 128], replicated, may hold values from -2.5 to 2.5
- occupancy: int32 [16, 16], replicated, may hold values 0 or 1
- row_gain: float32 [128], replicated, may hold values from 0.1 to 1.9
- row_qkv: bfloat16 [128, 384], replicated, may hold values from -5 to 5
- row_out: bfloat16 [128, 128], replicated, may hold values from -0.5 to 0.5
- col_gain: float32 [128], replicated, may hold values from 0.1 to 1.9
- col_qkv: bfloat16 [128, 384], replicated, may hold values from -5 to 5
- col_out: bfloat16 [128, 128], replicated, may hold values from -0.5 to 0.5
Outputs:
- mixed: bfloat16 [1024, 1024, 128], P(None, ('tile', 'slab'))
All inputs are finite; a program needn't handle non-finite values.
Results may differ from a plain program's by a relative error of at most 0.02.
Values may be sent and summed in bfloat16 or wider, within the bound.
A program may use at most 64 MiB of HBM per device.

v0:
```python
import math
import jax
import jax.numpy as jnp
from jax import lax
from jax.sharding import PartitionSpec as P

HEAD_DIM = 32
COL_REACH = 128


def padded_2(block, sides, width):
    for axis, dim in sides:
        count = lax.axis_size(axis)
        forward = [(i, i + 1) for i in range(count - 1)]
        backward = [(target, source) for source, target in forward]
        low = lax.ppermute(
            lax.slice_in_dim(block, block.shape[dim] - width, None, axis=dim), axis, forward
        )
        high = lax.ppermute(lax.slice_in_dim(block, 0, width, axis=dim), axis, backward)
        block = jnp.concatenate([low, block, high], axis=dim)
    return block


def attend(queries, key_block, value_block, query_pos, key_pos, query_ok, key_ok, band_reach):
    query_count = queries.shape[0]
    key_count = key_block.shape[0]
    head_count = queries.shape[1] // HEAD_DIM
    query_heads = queries.reshape(query_count, head_count, HEAD_DIM)
    key_heads = key_block.reshape(key_count, head_count, HEAD_DIM)
    value_heads = value_block.reshape(key_count, head_count, HEAD_DIM)
    scores = jnp.einsum(
        "qhd,khd->hqk", query_heads, key_heads, preferred_element_type=jnp.float32
    ) / math.sqrt(HEAD_DIM)
    offsets = query_pos[:, None] - key_pos[None, :]
    allowed = (jnp.abs(offsets) < band_reach) & ((key_ok[None, :] > 0) | (offsets == 0))
    scores = jnp.where(allowed[None], scores, jnp.float32(-1e30))
    row_max = jnp.max(scores, axis=-1, keepdims=True)
    exp_terms = jnp.exp(scores - row_max)
    row_total = jnp.sum(exp_terms, axis=-1, keepdims=True)
    weights = (exp_terms / row_total).astype(jnp.bfloat16)
    mixture = jnp.einsum("hqk,khd->qhd", weights, value_heads, preferred_element_type=jnp.float32)
    mixture = mixture * query_ok[:, None, None].astype(jnp.float32)
    return mixture.reshape(query_count, head_count * HEAD_DIM).astype(jnp.bfloat16)


def attend_line(projected, line_ok, band_reach):
    line_len = projected.shape[0]
    model_width = projected.shape[1] // 3
    block_rows = min(256, line_len)
    block_count = line_len // block_rows
    queries = projected[:, :model_width]
    key_value = jnp.pad(projected[:, model_width:], ((band_reach, band_reach), (0, 0)))
    padded_ok = jnp.pad(line_ok, (band_reach, band_reach))
    positions = jnp.arange(line_len + 2 * band_reach, dtype=jnp.int32) - band_reach

    def one_block(block_index):
        block_start = block_index * block_rows
        query_part = lax.dynamic_slice_in_dim(queries, block_start, block_rows, 0)
        query_ok = lax.dynamic_slice_in_dim(line_ok, block_start, block_rows, 0)
        query_pos = lax.dynamic_slice_in_dim(positions, block_start + band_reach, block_rows, 0)
        kv_part = lax.dynamic_slice_in_dim(key_value, block_start, block_rows + 2 * band_reach, 0)
        key_ok = lax.dynamic_slice_in_dim(padded_ok, block_start, block_rows + 2 * band_reach, 0)
        key_pos = lax.dynamic_slice_in_dim(positions, block_start, block_rows + 2 * band_reach, 0)
        return attend(
            query_part,
            kv_part[:, :model_width],
            kv_part[:, model_width:],
            query_pos,
            key_pos,
            query_ok,
            key_ok,
            band_reach,
        )

    blocks = lax.map(one_block, jnp.arange(block_count, dtype=jnp.int32))
    return blocks.reshape(line_len, model_width)


def layer_norm(stream, gain):
    values32 = stream.astype(jnp.float32)
    center = jnp.mean(values32, axis=-1, keepdims=True)
    centered = values32 - center
    spread = jnp.mean(centered * centered, axis=-1, keepdims=True)
    return (centered * lax.rsqrt(spread + 1e-05) * gain).astype(jnp.bfloat16)


def column_part(stream, col_ok, gain, qkv_weight, out_weight):
    normed = layer_norm(stream, gain)
    projected = jnp.dot(normed, qkv_weight, preferred_element_type=jnp.float32).astype(jnp.bfloat16)
    by_column = jnp.moveaxis(projected, 1, 0)
    ok_column = jnp.moveaxis(col_ok, 1, 0)
    mixture = lax.map(
        lambda pieces: attend_line(pieces[0], pieces[1], COL_REACH), (by_column, ok_column)
    )
    mixture = jnp.moveaxis(mixture, 0, 1)
    update = jnp.dot(mixture, out_weight, preferred_element_type=jnp.float32)
    return (stream.astype(jnp.float32) + update).astype(jnp.bfloat16)


def local(tokens, conv_weight, occupancy, row_gain, row_qkv, row_out, col_gain, col_qkv, col_out):
    row_count, length, model_width = tokens.shape
    slab_count = lax.axis_size("slab")
    slab_at = lax.axis_index("slab")
    tile_at = lax.axis_index("tile")
    height = row_count * slab_count
    block_size = height // occupancy.shape[0]
    band_reach = min(128, length)
    col_count = length // slab_count
    padded = padded_2(tokens, (("slab", 0), ("tile", 1)), 1)
    padded32 = padded.astype(jnp.float32)
    convolved = padded32[1 : 1 + row_count, 1 : 1 + length]
    for shift_row in range(3):
        for shift_col in range(3):
            convolved = (
                convolved
                + conv_weight[shift_row, shift_col]
                * padded32[shift_row : shift_row + row_count, shift_col : shift_col + length]
            )
    stream = convolved.astype(jnp.bfloat16)
    normed = layer_norm(stream, row_gain)
    projected = jnp.dot(normed, row_qkv, preferred_element_type=jnp.float32).astype(jnp.bfloat16)
    queries = projected[..., :model_width]
    line_ids = (slab_at * row_count + jnp.arange(row_count, dtype=jnp.int32)) // block_size
    selector = (
        line_ids[:, None] == jnp.arange(occupancy.shape[0], dtype=jnp.int32)[None, :]
    ).astype(jnp.int32)
    occ_rows = jnp.dot(selector, occupancy)
    occ_line = jnp.repeat(occ_rows, block_size, axis=1)
    occ_wide = jnp.pad(occ_line, ((0, 0), (band_reach, band_reach)))
    key_ok = lax.dynamic_slice_in_dim(occ_wide, tile_at * length, length + 2 * band_reach, 1)
    query_ok = key_ok[:, band_reach : band_reach + length]
    kv_wide = padded_2(projected[..., model_width:], (("tile", 1),), band_reach)
    query_pos = tile_at * length + jnp.arange(length, dtype=jnp.int32)
    key_pos = tile_at * length - band_reach + jnp.arange(length + 2 * band_reach, dtype=jnp.int32)

    def row_attend(pieces):
        query_row, kv_row, qok_row, kok_row = pieces
        return attend(
            query_row,
            kv_row[:, :model_width],
            kv_row[:, model_width:],
            query_pos,
            key_pos,
            qok_row,
            kok_row,
            band_reach,
        )

    mixture = lax.map(row_attend, (queries, kv_wide, query_ok, key_ok))
    after_rows = (
        stream.astype(jnp.float32) + jnp.dot(mixture, row_out, preferred_element_type=jnp.float32)
    ).astype(jnp.bfloat16)
    columns = lax.all_to_all(after_rows, "slab", split_axis=1, concat_axis=0, tiled=True)
    col_ids = (
        tile_at * length + slab_at * col_count + jnp.arange(col_count, dtype=jnp.int32)
    ) // block_size
    col_selector = (
        jnp.arange(occupancy.shape[1], dtype=jnp.int32)[:, None] == col_ids[None, :]
    ).astype(jnp.int32)
    occ_blocks = jnp.dot(occupancy, col_selector)
    col_ok = jnp.repeat(occ_blocks, block_size, axis=0)
    result = column_part(columns, col_ok, col_gain, col_qkv, col_out)
    return result


def solution(mesh):
    return jax.shard_map(
        local,
        mesh=mesh,
        in_specs=(P("slab", "tile", None), P(), P(), P(), P(), P(), P(), P(), P()),
        out_specs=P(None, ("tile", "slab"), None),
        check_vma=False,
    )
```

profile of v0, /device:TPU:1, one launch (start us, length us, event | category | flops | bytes accessed | tf_op | source)
XLA Modules:
  0.0 189.0 jit_solution(11534198888149711325)
XLA Ops:
  0.9 4.9 %collective-permute-start = (bf16[1,256,128]{2,1,0:T(8,128)(2,1)S(1)}, bf16[1,256,128]{2,1,0:T(8,128)(2,1)S(1)}, u32[]{:S(2)}, u32[]{:S(2)}) collective-permute-start(bf16[1,256,128]{2,1,0:T(8,128)(2,1)S(1)} %get-tuple-element.356), channel_id=1, source_target_pairs={{0,4},{4,8},{8,12},{12,16},{16,20},{20,24},{24,28},{28,32},{32,36}... | collective-permute-start | bytes 196616 | tf_op jit(solution)/shard_map/ppermute | solution.py:16
  5.9 5.1 %collective-permute-start.1 = (bf16[1,256,128]{2,1,0:T(8,128)(2,1)S(1)}, bf16[1,256,128]{2,1,0:T(8,128)(2,1)S(1)}, u32[]{:S(2)}, u32[]{:S(2)}) collective-permute-start(bf16[1,256,128]{2,1,0:T(8,128)(2,1)S(1)} %get-tuple-element.355), channel_id=1, source_target_pairs={{4,0},{8,4},{12,8},{16,12},{20,16},{24,20},{28,24},{32,28},{36,32}... | collective-permute-start | bytes 196616 | tf_op jit(solution)/shard_map/ppermute | solution.py:19
  11.0 1.1 constant_dynamic-update-slice_fusion.3
  12.2 2.4 %collective-permute-start.2 = (bf16[10,1,128]{2,1,0:T(2,128)(2,1)S(1)}, bf16[10,1,128]{2,1,0:T(2,128)(2,1)S(1)}, u32[]{:S(2)}, u32[]{:S(2)}) collective-permute-start(bf16[10,1,128]{2,1,0:T(2,128)(2,1)S(1)} %get-tuple-element.353), channel_id=1, source_target_pairs={{0,1},{1,2},{2,3},{4,5},{5,6},{6,7},{8,9},{9,10},{10,11},{12,13},{... | collective-permute-start | bytes 7688 | tf_op jit(solution)/shard_map/ppermute | solution.py:16
  14.6 1.3 collective-permute-start.3
  16.8 2.2 %collective-permute-done.3 = bf16[10,1,128]{2,1,0:T(2,128)(2,1)S(1)} collective-permute-done((bf16[10,1,128]{2,1,0:T(2,128)(2,1)S(1)}, bf16[10,1,128]{2,1,0:T(2,128)(2,1)S(1)}, u32[]{:S(2)}, u32[]{:S(2)}) %collective-permute-start.3) | collective-permute-done | bytes 2592 | tf_op jit(solution)/shard_map/ppermute | solution.py:19
  19.1 1.2 convert_reduce_fusion
  21.0 1.0 convolution_convert_fusion.1
  22.1 1.0 fusion.83
  23.0 3.9 %collective-permute-start.4 = (bf16[8,128,256]{2,1,0:T(8,128)(2,1)}, bf16[8,128,256]{2,1,0:T(8,128)(2,1)}, u32[]{:S(2)}, u32[]{:S(2)}) collective-permute-start(bf16[8,128,256]{2,1,0:T(8,128)(2,1)} %get-tuple-element.351), channel_id=1, source_target_pairs={{0,1},{1,2},{2,3},{4,5},{5,6},{6,7},{8,9},{9,10},{10,11},{12,13},{... | collective-permute-start | bytes 1572872 | tf_op jit(solution)/shard_map/ppermute | solution.py:16
  26.9 1.3 collective-permute-start.5
  28.8 8.9 %collective-permute-done.4 = bf16[8,128,256]{2,1,0:T(8,128)(2,1)} collective-permute-done((bf16[8,128,256]{2,1,0:T(8,128)(2,1)}, bf16[8,128,256]{2,1,0:T(8,128)(2,1)}, u32[]{:S(2)}, u32[]{:S(2)}) %collective-permute-start.4) | collective-permute-done | bytes 524320 | tf_op jit(solution)/shard_map/ppermute | solution.py:16
  37.7 4.7 %collective-permute-done.5 = bf16[8,128,256]{2,1,0:T(8,128)(2,1)} collective-permute-done((bf16[8,128,256]{2,1,0:T(8,128)(2,1)S(1)}, bf16[8,128,256]{2,1,0:T(8,128)(2,1)}, u32[]{:S(2)}, u32[]{:S(2)}) %collective-permute-start.5) | collective-permute-done | bytes 524320 | tf_op jit(solution)/shard_map/ppermute | solution.py:19
  42.4 2.7 %pad_maximum_fusion = bf16[8,512,256]{2,1,0:T(8,128)(2,1)} fusion(bf16[8,128,256]{2,1,0:T(8,128)(2,1)} %collective-permute-done.5, bf16[8,256,256]{2,1,0:T(8,128)(2,1)S(1)} %slice.161, bf16[8,128,256]{2,1,0:T(8,128)(2,1)} %collective-permute-done.4), kind=kLoop, calls=%fused_computation.61 | loop fusion | flops 6291456 | bytes 4194304 | tf_op jit(solution)/shard_map/concatenate | solution.py:20
  45.1 29.7 %while.45 = (s32[]{:T(128)}, bf16[8,256,128]{1,2,0:T(8,128)(2,1)S(1)}, bf16[8,512,256]{2,1,0:T(8,128)(2,1)}, s32[8,512]{1,0:T(8,128)S(1)}, bf16[8,256,128]{2,1,0...) while((s32[]{:T(128)}, bf16[8,256,128]{1,2,0:T(8,128)(2,1)S(1)}, ...), condition=%wide.region_5.6_spmd.clone, body=%wide.region_2.5_spmd.clone.sunk | while | flops 106237440 | bytes 2969721 | solution.py:149
  46.7 1.0 fusion.124
  47.7 1.1 fusion.126
  51.4 1.1 fusion.126
  55.1 1.1 fusion.126
  58.8 1.1 fusion.126
  62.5 1.1 fusion.126
  66.2 1.1 fusion.126
  69.9 1.1 fusion.126
  73.7 1.1 fusion.126
  75.1 1.1 copy.40
  76.3 19.1 %all-to-all-start = ((bf16[8,256,128]{2,0,1:T(8,128)(2,1)}), bf16[8,256,128]{2,0,1:T(8,128)(2,1)S(1)}, u32[]{:S(2)}, u32[]{:S(2)}) async-start(bf16[8,256,128]{2,0,1:T(8,128)(2,1)} %copy.40), calls=%async_computation | async-start | bytes 1048576 | tf_op jit(solution)/shard_map/all_to_all | solution.py:153
  95.7 32.8 %all-to-all-done = bf16[8,256,128]{2,0,1:T(8,128)(2,1)S(1)} async-done(((bf16[8,256,128]{2,0,1:T(8,128)(2,1)}), bf16[8,256,128]{2,0,1:T(8,128)(2,1)S(1)}, u32[]{:S(2)}, u32[]{:S(2)}) %all-to-all-start) | async-done | bytes 524320 | tf_op jit(solution)/shard_map/all_to_all | solution.py:153
  128.6 1.1 fusion.78
  129.8 1.5 copy.65
  131.9 14.7 %multiply_reduce_fusion = f32[128,8,2]{2,0,1:T(8,128)S(1)} fusion(f32[128,8,2]{2,0,1:T(8,128)S(1)} %copy.45, f32[8,128,2,128]{3,0,2,1:T(8,128)S(1)} %bitcast_convert_fusion), kind=kLoop, calls=%fused_computation.100 | loop fusion | flops 784384 | bytes 1064960 | tf_op jit(solution)/shard_map/reduce_sum | solution.py:83
  147.2 2.2 %fusion.41 = bf16[2,1024,384]{2,1,0:T(8,128)(2,1)S(1)} fusion(f32[128,8,2,128]{3,2,0,1:T(2,128)} %bitcast.154, f32[128]{0:T(128)S(1)} %copy-done.7, f32[1024,2]{0,1:T(2,128)S(1)} %rsqrt.21, f32[1024,2]{0,1:T(2,128)S(1)} %div.73, bf16[128,384]{1,0:T(8,128)(2,1)S(1)} %copy-done.2), kind=kOutput, calls=%fused_computation.67 | convolution fusion | flops 203161600 | bytes 2736640 | tf_op jit(solution)/shard_map/dot_general | solution.py:89
  149.4 36.1 %while.44 = (s32[]{:T(128)}, bf16[2,1024,128]{2,1,0:T(8,128)(2,1)}, bf16[2,1024,384]{2,1,0:T(8,128)(2,1)S(1)}, s32[2,1024]{1,0:T(2,128)S(1)}, s32[]{:T(128)}, /*...) while((s32[]{:T(128)}, bf16[2,1024,128]{2,1,0:T(8,128)(2,1)}, ...), condition=%wide.region_13.14_spmd, body=%wide.region_8.13_spmd.sunk | while | flops 106237968 | bytes 8370293 | solution.py:92
  150.0 16.7 %while.46 = (s32[]{:T(128)}, bf16[4,256,128]{2,1,0:T(8,128)(2,1)S(1)}, s32[4]{0:T(128)S(1)}, bf16[1280,256]{0,1:T(8,128)(2,1)S(1)}, s32[1280]{0:T(1024)S(1)}, /*...) while((s32[]{:T(128)}, ...), condition=%wide.region_12.12_spmd.clone, body=%wide.region_9.11_spmd.clone.sunk | while | flops 106236688 | bytes 1924418 | solution.py:75
  152.9 1.1 fusion.134
  157.1 1.1 fusion.134
  161.3 1.1 fusion.134
  165.5 1.1 fusion.134
  168.1 16.7 %while.46 = (s32[]{:T(128)}, bf16[4,256,128]{2,1,0:T(8,128)(2,1)S(1)}, s32[4]{0:T(128)S(1)}, bf16[1280,256]{0,1:T(8,128)(2,1)S(1)}, s32[1280]{0:T(1024)S(1)}, /*...) while((s32[]{:T(128)}, ...), condition=%wide.region_12.12_spmd.clone, body=%wide.region_9.11_spmd.clone.sunk | while | flops 106236688 | bytes 1924418 | solution.py:75
  170.0 1.0 fusion.133
  171.0 1.1 fusion.134
  174.1 1.0 fusion.133
  175.2 1.1 fusion.134
  178.3 1.0 fusion.133
  179.4 1.1 fusion.134
  182.5 1.0 fusion.133
  183.6 1.1 fusion.134
  185.5 2.1 %fusion.43 = bf16[1024,2,128]{2,0,1:T(8,128)(2,1)S(1)} fusion(f32[128,8,2,128]{3,2,0,1:T(2,128)} %bitcast.155, bf16[2,1024,128]{2,1,0:T(8,128)(2,1)} %get-tuple-element.223, bf16[128,128]{1,0:T(8,128)(2,1)S(1)} %copy-done.3), kind=kOutput, calls=%fused_computation.70 | convolution fusion | flops 67633152 | bytes 2129920 | tf_op jit(solution)/shard_map/dot_general | solution.py:96
  187.7 1.3 copy.49
  (255 shorter events, 42.5 us)
Async XLA Ops:
  0.0 21.0 %copy-start = (bf16[128,384]{1,0:T(8,128)(2,1)S(1)}, bf16[128,384]{1,0:T(8,128)(2,1)}, u32[]{:S(2)}) copy-start(bf16[128,384]{1,0:T(8,128)(2,1)} %param.19) | copy-start | bytes 294916
  0.9 10.1 %collective-permute-start = (bf16[1,256,128]{2,1,0:T(8,128)(2,1)S(1)}, bf16[1,256,128]{2,1,0:T(8,128)(2,1)S(1)}, u32[]{:S(2)}, u32[]{:S(2)}) collective-permute-start(bf16[1,256,128]{2,1,0:T(8,128)(2,1)S(1)} %get-tuple-element.356), channel_id=1, source_target_pairs={{0,4},{4,8},{8,12},{12,16},{16,20},{20,24},{24,28},{28,32},{32,36}... | collective-permute-start | bytes 196616 | tf_op jit(solution)/shard_map/ppermute | solution.py:16
  5.9 6.3 %collective-permute-start.1 = (bf16[1,256,128]{2,1,0:T(8,128)(2,1)S(1)}, bf16[1,256,128]{2,1,0:T(8,128)(2,1)S(1)}, u32[]{:S(2)}, u32[]{:S(2)}) collective-permute-start(bf16[1,256,128]{2,1,0:T(8,128)(2,1)S(1)} %get-tuple-element.355), channel_id=1, source_target_pairs={{4,0},{8,4},{12,8},{16,12},{20,16},{24,20},{28,24},{32,28},{36,32}... | collective-permute-start | bytes 196616 | tf_op jit(solution)/shard_map/ppermute | solution.py:19
  12.2 4.6 %collective-permute-start.2 = (bf16[10,1,128]{2,1,0:T(2,128)(2,1)S(1)}, bf16[10,1,128]{2,1,0:T(2,128)(2,1)S(1)}, u32[]{:S(2)}, u32[]{:S(2)}) collective-permute-start(bf16[10,1,128]{2,1,0:T(2,128)(2,1)S(1)} %get-tuple-element.353), channel_id=1, source_target_pairs={{0,1},{1,2},{2,3},{4,5},{5,6},{6,7},{8,9},{9,10},{10,11},{12,13},{... | collective-permute-start | bytes 7688 | tf_op jit(solution)/shard_map/ppermute | solution.py:16
  14.6 4.4 %collective-permute-start.3 = (bf16[10,1,128]{2,1,0:T(2,128)(2,1)S(1)}, bf16[10,1,128]{2,1,0:T(2,128)(2,1)S(1)}, u32[]{:S(2)}, u32[]{:S(2)}) collective-permute-start(bf16[10,1,128]{2,1,0:T(2,128)(2,1)S(1)} %get-tuple-element.354), channel_id=1, source_target_pairs={{1,0},{2,1},{3,2},{5,4},{6,5},{7,6},{9,8},{10,9},{11,10},{13,12},{... | collective-permute-start | bytes 7688 | tf_op jit(solution)/shard_map/ppermute | solution.py:19
  19.1 1.9 copy-start.6
  21.0 7.3 %copy-start.5 = (s32[16,16]{1,0:T(8,128)S(1)}, s32[16,16]{1,0:T(8,128)}, u32[]{:S(2)}) copy-start(s32[16,16]{1,0:T(8,128)} %param.17) | copy-start | bytes 3076
  22.1 6.7 %copy-start.1 = (bf16[8,256,384]{2,1,0:T(8,128)(2,1)}, bf16[8,256,384]{2,1,0:T(8,128)(2,1)S(1)}, u32[]{:S(2)}) copy-start(bf16[8,256,384]{2,1,0:T(8,128)(2,1)S(1)} %convolution_convert_fusion.1) | copy-start | bytes 4718596
  23.0 14.6 %collective-permute-start.4 = (bf16[8,128,256]{2,1,0:T(8,128)(2,1)}, bf16[8,128,256]{2,1,0:T(8,128)(2,1)}, u32[]{:S(2)}, u32[]{:S(2)}) collective-permute-start(bf16[8,128,256]{2,1,0:T(8,128)(2,1)} %get-tuple-element.351), channel_id=1, source_target_pairs={{0,1},{1,2},{2,3},{4,5},{5,6},{6,7},{8,9},{9,10},{10,11},{12,13},{... | collective-permute-start | bytes 1572872 | tf_op jit(solution)/shard_map/ppermute | solution.py:16
  26.9 15.4 %collective-permute-start.5 = (bf16[8,128,256]{2,1,0:T(8,128)(2,1)S(1)}, bf16[8,128,256]{2,1,0:T(8,128)(2,1)}, u32[]{:S(2)}, u32[]{:S(2)}) collective-permute-start(bf16[8,128,256]{2,1,0:T(8,128)(2,1)S(1)} %get-tuple-element.352), channel_id=1, source_target_pairs={{1,0},{2,1},{3,2},{5,4},{6,5},{7,6},{9,8},{10,9},{11,10},{13,12},{... | collective-permute-start | bytes 1572872 | tf_op jit(solution)/shard_map/ppermute | solution.py:19
  28.7 16.3 %slice-start = ((bf16[8,256,384]{2,1,0:T(8,128)(2,1)}), bf16[8,256,128]{2,1,0:T(8,128)(2,1)S(1)}, s32[]{:S(2)}) async-start(bf16[8,256,384]{2,1,0:T(8,128)(2,1)} %copy-done.1), calls=%async_computation.1 | async-start | bytes 1048576 | tf_op jit(solution)/shard_map/slice | solution.py:122
  45.1 29.7 %copy-start.4 = (bf16[128,128]{1,0:T(8,128)(2,1)S(1)}, bf16[128,128]{1,0:T(8,128)(2,1)}, u32[]{:S(2)}) copy-start(bf16[128,128]{1,0:T(8,128)(2,1)} %param.20) | copy-start | bytes 98308
  76.3 52.3 %all-to-all-start = ((bf16[8,256,128]{2,0,1:T(8,128)(2,1)}), bf16[8,256,128]{2,0,1:T(8,128)(2,1)S(1)}, u32[]{:S(2)}, u32[]{:S(2)}) async-start(bf16[8,256,128]{2,0,1:T(8,128)(2,1)} %copy.40), calls=%async_computation | async-start | bytes 1048576 | tf_op jit(solution)/shard_map/all_to_all | solution.py:153
  131.3 15.9 %copy-start.2 = (bf16[128,384]{1,0:T(8,128)(2,1)S(1)}, bf16[128,384]{1,0:T(8,128)(2,1)}, u32[]{:S(2)}) copy-start(bf16[128,384]{1,0:T(8,128)(2,1)} %param.22) | copy-start | bytes 294916
  131.3 15.9 %copy-start.7 = (f32[128]{0:T(128)S(1)}, f32[128]{0:T(128)}, u32[]{:S(2)}) copy-start(f32[128]{0:T(128)} %param.21) | copy-start | bytes 1540
  149.4 36.2 %copy-start.3 = (bf16[128,128]{1,0:T(8,128)(2,1)S(1)}, bf16[128,128]{1,0:T(8,128)(2,1)}, u32[]{:S(2)}) copy-start(bf16[128,128]{1,0:T(8,128)(2,1)} %param.23) | copy-start | bytes 98308
where the time goes:
time: 190 us; the launch traced here: 189 us
  waiting for transfers between devices  48.6 us (26%)
  matrix products  38.5 us (20%)
  starting transfers between devices  38 us (20%)
  local copies, waits for them, and re-layouts  30.4 us (16%)
  other arithmetic  26.6 us (14%)
  loops' own time  6.54 us (3%)
    all_to_all x1, waiting for transfers between devices, local(): lax.all_to_all(after_rows, 'slab', split_axis=1, concat_axis=0, tiled=True)  32.8 us
    all_to_all x1, starting transfers between devices, local(): lax.all_to_all(after_rows, 'slab', split_axis=1, concat_axis=0, tiled=True)  19.1 us
    dot_general x16, matrix products, attend(): jnp.einsum('hqk,khd->qhd', weights, value_heads, preferred_element_type=j...  16.9 us
    sub x16, matrix products, attend(): exp_terms = jnp.exp(scores - row_max)  15.5 us
    reduce_sum x2, other arithmetic, layer_norm(): spread = jnp.mean(centered * centered, axis=-1, keepdims=True)  15.4 us
    ppermute x3, starting transfers between devices, padded_2(): lax.ppermute(lax.slice_in_dim(block, block.shape[dim] - width, None, axis...  11.2 us
    dynamic_slice x32, local copies, waits for them, and re-layouts, local(): mixture = lax.map(row_attend, (queries, kv_wide, query_ok, key_ok))  9.88 us
    ppermute x3, waiting for transfers between devices, padded_2(): lax.ppermute(lax.slice_in_dim(block, block.shape[dim] - width, None, axis...  8.91 us
  transfers between devices with their start and end apart: 7, of which 4 were waited for; matrix products, arithmetic and copies ran while one was open for 1% of the time, Pallas kernels for 0%

commit v1 on v0

--- a/solution.py
+++ b/solution.py
@@ -150,7 +150,12 @@
     after_rows = (
         stream.astype(jnp.float32) + jnp.dot(mixture, row_out, preferred_element_type=jnp.float32)
     ).astype(jnp.bfloat16)
-    columns = lax.all_to_all(after_rows, "slab", split_axis=1, concat_axis=0, tiled=True)
+    columns = jnp.concatenate(
+        lax.all_to_all(
+            jnp.stack(jnp.split(after_rows, lax.axis_size("slab"), axis=1)), "slab", 0, 0
+        ),
+        axis=0,
+    )
     col_ids = (
         tile_at * length + slab_at * col_count + jnp.arange(col_count, dtype=jnp.int32)
     ) // block_size

time: 190 us -> 252 us (1.33)
  local copies, waits for them, and re-layouts: 30.4 us -> 103 us
  other arithmetic: 26.6 us -> 18.5 us
    unnamed x18 -> x147, local copies, waits for them, and re-layouts: 1.16 us -> 77.4 us
    reduce_sum x2, other arithmetic: 15.4 us -> 3.36 us  [layer_norm(): spread = jnp.mean(centered * centered, axis=-1, keepdims=True)]
where the time goes in v1:
time: 252 us
  local copies, waits for them, and re-layouts  103 us (41%)
  waiting for transfers between devices  48.6 us (19%)
  starting transfers between devices  38 us (15%)
  matrix products  36.2 us (14%)
  other arithmetic  18.5 us (7%)
  loops' own time  6.95 us (3%)
    unnamed x147, local copies, waits for them, and re-layouts  77.4 us
    all_to_all x1, waiting for transfers between devices, local(): lax.all_to_all(jnp.stack(jnp.split(after_rows, lax.axis_size('slab'), axi...  32.8 us
    all_to_all x1, starting transfers between devices, local(): lax.all_to_all(jnp.stack(jnp.split(after_rows, lax.axis_size('slab'), axi...  19.1 us
    dot_general x16, matrix products, attend(): jnp.einsum('hqk,khd->qhd', weights, value_heads, preferred_element_type=j...  17 us
    sub x16, matrix products, attend(): exp_terms = jnp.exp(scores - row_max)  15.5 us
    ppermute x3, starting transfers between devices, padded_2(): lax.ppermute(lax.slice_in_dim(block, block.shape[dim] - width, None, axis...  11.2 us
    dynamic_slice x32, local copies, waits for them, and re-layouts, local(): mixture = lax.map(row_attend, (queries, kv_wide, query_ok, key_ok))  9.88 us
    ppermute x3, waiting for transfers between devices, padded_2(): lax.ppermute(lax.slice_in_dim(block, block.shape[dim] - width, None, axis...  8.91 us
  transfers between devices with their start and end apart: 7, of which 4 were waited for; matrix products, arithmetic and copies ran while one was open for 1% of the time, Pallas kernels for 0%

profile of v1, /device:TPU:1, one launch (start us, length us, event | category | flops | bytes accessed | tf_op | source)
XLA Modules:
  0.0 251.6 jit_solution(4308076617421250878)
XLA Ops:
  0.9 4.9 %collective-permute-start = (bf16[1,256,128]{2,1,0:T(8,128)(2,1)S(1)}, bf16[1,256,128]{2,1,0:T(8,128)(2,1)S(1)}, u32[]{:S(2)}, u32[]{:S(2)}) collective-permute-start(bf16[1,256,128]{2,1,0:T(8,128)(2,1)S(1)} %get-tuple-element.326), channel_id=1, source_target_pairs={{0,4},{4,8},{8,12},{12,16},{16,20},{20,24},{24,28},{28,32},{32,36}... | collective-permute-start | bytes 196616 | tf_op jit(solution)/shard_map/ppermute | solution.py:16
  5.9 5.1 %collective-permute-start.1 = (bf16[1,256,128]{2,1,0:T(8,128)(2,1)S(1)}, bf16[1,256,128]{2,1,0:T(8,128)(2,1)S(1)}, u32[]{:S(2)}, u32[]{:S(2)}) collective-permute-start(bf16[1,256,128]{2,1,0:T(8,128)(2,1)S(1)} %get-tuple-element.325), channel_id=1, source_target_pairs={{4,0},{8,4},{12,8},{16,12},{20,16},{24,20},{28,24},{32,28},{36,32}... | collective-permute-start | bytes 196616 | tf_op jit(solution)/shard_map/ppermute | solution.py:19
  11.0 1.1 constant_dynamic-update-slice_fusion.3
  12.2 2.4 collective-permute-start.2
  14.6 1.3 collective-permute-start.3
  16.8 2.2 collective-permute-done.3
  19.1 1.2 convert_reduce_fusion
  21.0 1.0 convolution_convert_fusion.1
  22.1 1.0 fusion.77
  23.0 3.9 %collective-permute-start.4 = (bf16[8,128,256]{2,1,0:T(8,128)(2,1)}, bf16[8,128,256]{2,1,0:T(8,128)(2,1)}, u32[]{:S(2)}, u32[]{:S(2)}) collective-permute-start(bf16[8,128,256]{2,1,0:T(8,128)(2,1)} %get-tuple-element.319), channel_id=1, source_target_pairs={{0,1},{1,2},{2,3},{4,5},{5,6},{6,7},{8,9},{9,10},{10,11},{12,13},{... | collective-permute-start | bytes 1572872 | tf_op jit(solution)/shard_map/ppermute | solution.py:16
  26.9 1.3 collective-permute-start.5
  28.8 8.9 %collective-permute-done.4 = bf16[8,128,256]{2,1,0:T(8,128)(2,1)} collective-permute-done((bf16[8,128,256]{2,1,0:T(8,128)(2,1)}, bf16[8,128,256]{2,1,0:T(8,128)(2,1)}, u32[]{:S(2)}, u32[]{:S(2)}) %collective-permute-start.4) | collective-permute-done | bytes 524320 | tf_op jit(solution)/shard_map/ppermute | solution.py:16
  37.7 4.7 %collective-permute-done.5 = bf16[8,128,256]{2,1,0:T(8,128)(2,1)} collective-permute-done((bf16[8,128,256]{2,1,0:T(8,128)(2,1)S(1)}, bf16[8,128,256]{2,1,0:T(8,128)(2,1)}, u32[]{:S(2)}, u32[]{:S(2)}) %collective-permute-start.5) | collective-permute-done | bytes 524320 | tf_op jit(solution)/shard_map/ppermute | solution.py:19
  42.4 2.7 %pad_maximum_fusion = bf16[8,512,256]{2,1,0:T(8,128)(2,1)} fusion(bf16[8,128,256]{2,1,0:T(8,128)(2,1)} %collective-permute-done.5, bf16[8,256,256]{2,1,0:T(8,128)(2,1)S(1)} %slice.161, bf16[8,128,256]{2,1,0:T(8,128)(2,1)} %collective-permute-done.4), kind=kLoop, calls=%fused_computation.61 | loop fusion | flops 6291456 | bytes 4194304 | tf_op jit(solution)/shard_map/concatenate | solution.py:20
  45.1 29.7 %while.45 = (s32[]{:T(128)}, bf16[8,256,128]{1,2,0:T(8,128)(2,1)S(1)}, bf16[8,512,256]{2,1,0:T(8,128)(2,1)}, s32[8,512]{1,0:T(8,128)S(1)}, bf16[8,256,128]{2,1,0...) while((s32[]{:T(128)}, bf16[8,256,128]{1,2,0:T(8,128)(2,1)S(1)}, ...), condition=%wide.region_5.6_spmd.clone, body=%wide.region_2.5_spmd.clone.sunk | while | flops 106237440 | bytes 2969721 | solution.py:149
  46.7 1.0 fusion.118
  47.7 1.1 fusion.120
  51.4 1.1 fusion.120
  55.1 1.1 fusion.120
  58.8 1.1 fusion.120
  62.5 1.1 fusion.120
  66.2 1.1 fusion.120
  69.9 1.1 fusion.120
  73.7 1.1 fusion.120
  152.0 19.1 %all-to-all-start = ((bf16[128,8,2,128]{3,2,1,0:T(2,128)(2,1)}), bf16[128,8,2,128]{3,2,1,0:T(2,128)(2,1)S(1)}, u32[]{:S(2)}, u32[]{:S(2)}) async-start(bf16[128,8,2,128]{3,2,1,0:T(2,128)(2,1)} %constant_dynamic-update-slice_fusion.5), calls=%async_computation | async-start | bytes 1048576 | tf_op jit(solution)/shard_map/all_to_all | solution.py:154
  171.5 32.8 %all-to-all-done = bf16[128,8,2,128]{3,2,1,0:T(2,128)(2,1)S(1)} async-done(((bf16[128,8,2,128]{3,2,1,0:T(2,128)(2,1)}), bf16[128,8,2,128]{3,2,1,0:T(2,128)(2,1)S(1)}, u32[]{:S(2)}, u32[]{:S(2)}) %all-to-all-start) | async-done | bytes 524320 | tf_op jit(solution)/shard_map/all_to_all | solution.py:154
  204.3 1.2 convert_reduce_fusion.1
  205.5 2.7 %multiply_reduce_fusion = f32[128,8,2]{2,1,0:T(8,128)S(1)} fusion(bf16[128,8,2,128]{3,2,1,0:T(2,128)(2,1)S(1)} %all-to-all-done, f32[128,8,2]{2,1,0:T(8,128)S(1)} %get-tuple-element.324), kind=kLoop, calls=%fused_computation.96 | loop fusion | flops 1046528 | bytes 540672 | tf_op jit(solution)/shard_map/reduce_sum | solution.py:83
  208.4 2.5 multiply_convert_fusion
  211.5 36.1 %while.44 = (s32[]{:T(128)}, bf16[2,1024,128]{2,1,0:T(8,128)(2,1)}, bf16[2,1024,384]{1,2,0:T(8,128)(2,1)S(1)}, s32[2,1024]{1,0:T(2,128)S(1)}, s32[]{:T(128)}, /*...) while((s32[]{:T(128)}, bf16[2,1024,128]{2,1,0:T(8,128)(2,1)}, ...), condition=%wide.region_13.14_spmd, body=%wide.region_8.13_spmd.sunk | while | flops 106237968 | bytes 6797429 | solution.py:92
  211.8 17.0 %while.46 = (s32[]{:T(128)}, bf16[4,256,128]{2,1,0:T(8,128)(2,1)S(1)}, s32[4]{0:T(128)S(1)}, bf16[1280,256]{0,1:T(8,128)(2,1)S(1)}, s32[1280]{0:T(1024)S(1)}, /*...) while((s32[]{:T(128)}, ...), condition=%wide.region_12.12_spmd.clone, body=%wide.region_9.11_spmd.clone.sunk | while | flops 106236688 | bytes 1924418 | solution.py:75
  213.7 1.0 fusion.127
  214.8 1.1 fusion.128
  219.1 1.1 fusion.128
  222.3 1.0 fusion.127
  223.3 1.1 fusion.128
  226.5 1.0 fusion.127
  227.6 1.1 fusion.128
  229.8 17.0 %while.46 = (s32[]{:T(128)}, bf16[4,256,128]{2,1,0:T(8,128)(2,1)S(1)}, s32[4]{0:T(128)S(1)}, bf16[1280,256]{0,1:T(8,128)(2,1)S(1)}, s32[1280]{0:T(1024)S(1)}, /*...) while((s32[]{:T(128)}, ...), condition=%wide.region_12.12_spmd.clone, body=%wide.region_9.11_spmd.clone.sunk | while | flops 106236688 | bytes 1924418 | solution.py:75
  231.8 1.0 fusion.127
  232.8 1.1 fusion.128
  237.1 1.1 fusion.128
  241.3 1.1 fusion.128
  244.5 1.0 fusion.127
  245.6 1.1 fusion.128
  247.6 1.4 bitcast_convert_fusion
  249.0 1.3 fusion.43
  250.3 1.3 copy.15
  (375 shorter events, 117.4 us)
Async XLA Ops:
  0.0 21.0 %copy-start = (bf16[128,384]{1,0:T(8,128)(2,1)S(1)}, bf16[128,384]{1,0:T(8,128)(2,1)}, u32[]{:S(2)}) copy-start(bf16[128,384]{1,0:T(8,128)(2,1)} %param.19) | copy-start | bytes 294916
  0.9 10.1 %collective-permute-start = (bf16[1,256,128]{2,1,0:T(8,128)(2,1)S(1)}, bf16[1,256,128]{2,1,0:T(8,128)(2,1)S(1)}, u32[]{:S(2)}, u32[]{:S(2)}) collective-permute-start(bf16[1,256,128]{2,1,0:T(8,128)(2,1)S(1)} %get-tuple-element.326), channel_id=1, source_target_pairs={{0,4},{4,8},{8,12},{12,16},{16,20},{20,24},{24,28},{28,32},{32,36}... | collective-permute-start | bytes 196616 | tf_op jit(solution)/shard_map/ppermute | solution.py:16
  5.9 6.3 %collective-permute-start.1 = (bf16[1,256,128]{2,1,0:T(8,128)(2,1)S(1)}, bf16[1,256,128]{2,1,0:T(8,128)(2,1)S(1)}, u32[]{:S(2)}, u32[]{:S(2)}) collective-permute-start(bf16[1,256,128]{2,1,0:T(8,128)(2,1)S(1)} %get-tuple-element.325), channel_id=1, source_target_pairs={{4,0},{8,4},{12,8},{16,12},{20,16},{24,20},{28,24},{32,28},{36,32}... | collective-permute-start | bytes 196616 | tf_op jit(solution)/shard_map/ppermute | solution.py:19
  12.2 4.6 %collective-permute-start.2 = (bf16[10,1,128]{2,1,0:T(2,128)(2,1)S(1)}, bf16[10,1,128]{2,1,0:T(2,128)(2,1)S(1)}, u32[]{:S(2)}, u32[]{:S(2)}) collective-permute-start(bf16[10,1,128]{2,1,0:T(2,128)(2,1)S(1)} %get-tuple-element.321), channel_id=1, source_target_pairs={{0,1},{1,2},{2,3},{4,5},{5,6},{6,7},{8,9},{9,10},{10,11},{12,13},{... | collective-permute-start | bytes 7688 | tf_op jit(solution)/shard_map/ppermute | solution.py:16
  14.6 4.4 %collective-permute-start.3 = (bf16[10,1,128]{2,1,0:T(2,128)(2,1)S(1)}, bf16[10,1,128]{2,1,0:T(2,128)(2,1)S(1)}, u32[]{:S(2)}, u32[]{:S(2)}) collective-permute-start(bf16[10,1,128]{2,1,0:T(2,128)(2,1)S(1)} %get-tuple-element.322), channel_id=1, source_target_pairs={{1,0},{2,1},{3,2},{5,4},{6,5},{7,6},{9,8},{10,9},{11,10},{13,12},{... | collective-permute-start | bytes 7688 | tf_op jit(solution)/shard_map/ppermute | solution.py:19
  19.1 1.9 copy-start.7
  21.0 7.3 %copy-start.6 = (s32[16,16]{1,0:T(8,128)S(1)}, s32[16,16]{1,0:T(8,128)}, u32[]{:S(2)}) copy-start(s32[16,16]{1,0:T(8,128)} %param.17) | copy-start | bytes 3076
  22.1 6.7 %copy-start.2 = (bf16[8,256,384]{2,1,0:T(8,128)(2,1)}, bf16[8,256,384]{2,1,0:T(8,128)(2,1)S(1)}, u32[]{:S(2)}) copy-start(bf16[8,256,384]{2,1,0:T(8,128)(2,1)S(1)} %convolution_convert_fusion.1) | copy-start | bytes 4718596
  23.0 14.6 %collective-permute-start.4 = (bf16[8,128,256]{2,1,0:T(8,128)(2,1)}, bf16[8,128,256]{2,1,0:T(8,128)(2,1)}, u32[]{:S(2)}, u32[]{:S(2)}) collective-permute-start(bf16[8,128,256]{2,1,0:T(8,128)(2,1)} %get-tuple-element.319), channel_id=1, source_target_pairs={{0,1},{1,2},{2,3},{4,5},{5,6},{6,7},{8,9},{9,10},{10,11},{12,13},{... | collective-permute-start | bytes 1572872 | tf_op jit(solution)/shard_map/ppermute | solution.py:16
  26.9 15.4 %collective-permute-start.5 = (bf16[8,128,256]{2,1,0:T(8,128)(2,1)S(1)}, bf16[8,128,256]{2,1,0:T(8,128)(2,1)}, u32[]{:S(2)}, u32[]{:S(2)}) collective-permute-start(bf16[8,128,256]{2,1,0:T(8,128)(2,1)S(1)} %get-tuple-element.320), channel_id=1, source_target_pairs={{1,0},{2,1},{3,2},{5,4},{6,5},{7,6},{9,8},{10,9},{11,10},{13,12},{... | collective-permute-start | bytes 1572872 | tf_op jit(solution)/shard_map/ppermute | solution.py:19
  28.7 16.3 %slice-start = ((bf16[8,256,384]{2,1,0:T(8,128)(2,1)}), bf16[8,256,128]{2,1,0:T(8,128)(2,1)S(1)}, s32[]{:S(2)}) async-start(bf16[8,256,384]{2,1,0:T(8,128)(2,1)} %copy-done.2), calls=%async_computation.1 | async-start | bytes 1048576 | tf_op jit(solution)/shard_map/slice | solution.py:122
  45.1 29.7 %copy-start.5 = (bf16[128,128]{1,0:T(8,128)(2,1)S(1)}, bf16[128,128]{1,0:T(8,128)(2,1)}, u32[]{:S(2)}) copy-start(bf16[128,128]{1,0:T(8,128)(2,1)} %param.20) | copy-start | bytes 98308
  152.0 52.3 %all-to-all-start = ((bf16[128,8,2,128]{3,2,1,0:T(2,128)(2,1)}), bf16[128,8,2,128]{3,2,1,0:T(2,128)(2,1)S(1)}, u32[]{:S(2)}, u32[]{:S(2)}) async-start(bf16[128,8,2,128]{3,2,1,0:T(2,128)(2,1)} %constant_dynamic-update-slice_fusion.5), calls=%async_computation | async-start | bytes 1048576 | tf_op jit(solution)/shard_map/all_to_all | solution.py:154
  204.3 4.1 %copy-start.1 = (bf16[128,8,2,128]{3,2,1,0:T(2,128)(2,1)}, bf16[128,8,2,128]{3,2,1,0:T(2,128)(2,1)S(1)}, u32[]{:S(2)}) copy-start(bf16[128,8,2,128]{3,2,1,0:T(2,128)(2,1)S(1)} %all-to-all-done) | copy-start | bytes 1572868
  205.4 2.9 %copy-start.8 = (f32[128]{0:T(128)S(1)}, f32[128]{0:T(128)}, u32[]{:S(2)}) copy-start(f32[128]{0:T(128)} %param.21) | copy-start | bytes 1540
  205.5 5.3 %copy-start.3 = (bf16[128,384]{1,0:T(8,128)(2,1)S(1)}, bf16[128,384]{1,0:T(8,128)(2,1)}, u32[]{:S(2)}) copy-start(bf16[128,384]{1,0:T(8,128)(2,1)} %param.22) | copy-start | bytes 294916
  211.5 37.5 %copy-start.4 = (bf16[128,128]{1,0:T(8,128)(2,1)S(1)}, bf16[128,128]{1,0:T(8,128)(2,1)}, u32[]{:S(2)}) copy-start(bf16[128,128]{1,0:T(8,128)(2,1)} %param.23) | copy-start | bytes 98308
